TPU v7x, 512 devices: a whole 4x4x16 slice. The times are simulated.
512 devices in a mesh: row: 16 (over y_lo, x, core), col: 32 (over z, y_hi).
Axes of the slice: x: 4, y: 4 (y_hi: 2, y_lo: 2; y = y_hi * 2 + y_lo), z: 16, core: 2. Of those that a mesh axis runs over, the one named last changes fastest.
Arguments:
- amplitudes: bfloat16 [32768, 16384], P('row', 'col'), may hold values from -6 to 6
- integrals: bfloat16 [16384, 2048], P('col'), may hold values from -0.125 to 0.125
- pair_index: int32 [32768], P('row'), may hold values from 0 to 39999, as said below
- partner: int32 [32768], P('row'), may hold values from 0 to 32767, as said below
- occ_energy: float32 [200], replicated, may hold values from -1 to -0.3
- vir_energy: float32 [2000], replicated, may hold values from 0.05 to 1
Outputs:
- increment: bfloat16 [32768, 16384], P('row', 'col')
Inputs may be any that keep to these rules, and one draw needn't show every extreme that they name: `pair_index`: rows 0 and 1 hold the pairs (199, 199) and (0, 0); otherwise i and j are independent and uniform over 0 to 199. partner is an involution; partner[k] lies in row block (k // 2048) XOR (8), and pair_index[partner[k]] is pair_index[k] with i and j exchanged.
All inputs are finite; a program needn't handle non-finite values.
Results may differ from a plain program's by a relative error of at most 0.001.
Values may be sent and summed in bfloat16 or wider, within the bound.
A program may use at most 128 MiB of HBM per device.

v0:
```python
import jax
import jax.numpy as jnp
from jax import lax
from jax.sharding import PartitionSpec as P

NOCC = 200
NV = 2000


def passed_along(value, axis, steps):
    count = lax.axis_size(axis)
    pairs = [(source, (source + steps) % count) for source in range(count)]
    return lax.ppermute(value, axis, pairs)


def partner_2(x, axis, apart):
    return lax.ppermute(x, axis, [(i, i ^ 1 << apart) for i in range(lax.axis_size(axis))])


def mirror_pairs(values):
    pair_width = values.shape[1]
    parity = jnp.arange(pair_width, dtype=jnp.int32) % 2 == 0
    return jnp.where(parity[None, :], jnp.roll(values, -1, axis=1), jnp.roll(values, 1, axis=1))


def table_lookup(table, positions):
    slots = jnp.arange(table.shape[0], dtype=jnp.int32)
    return jnp.sum(jnp.where(positions[:, None] == slots[None, :], table[None, :], 0.0), axis=1)


def contract_stops(amp_rows, integrals, pair_width):
    stop_count = integrals.shape[1] // pair_width
    running = jnp.dot(amp_rows, integrals[:, :pair_width], preferred_element_type=jnp.float32)
    slab_rest = integrals[:, pair_width:]
    moving = amp_rows
    for stop_index in range(1, stop_count):
        slab_rest, moving = passed_along((slab_rest, moving), "col", 1)
        running = running + jnp.dot(
            moving, slab_rest[:, :pair_width], preferred_element_type=jnp.float32
        )
        slab_rest = slab_rest[:, pair_width:]
    return running


def shards(amplitudes, integrals, pair_index, partner, occ_energy, vir_energy):
    row_count, pair_width = amplitudes.shape
    bit_number = lax.axis_size("row").bit_length() - 2
    local_partner = partner % row_count
    running = contract_stops(amplitudes, integrals, pair_width)
    partner_sums = partner_2(running, "row", bit_number)
    opposite = jnp.take(partner_sums, local_partner, axis=0)
    summed = running + mirror_pairs(opposite)
    occ_sum = table_lookup(occ_energy, pair_index // NOCC) + table_lookup(
        occ_energy, pair_index % NOCC
    )
    global_pair = lax.axis_index("col") * pair_width + jnp.arange(pair_width, dtype=jnp.int32)
    unordered = global_pair // 2
    vir_sum = table_lookup(vir_energy, unordered // NV) + table_lookup(vir_energy, unordered % NV)
    denom = vir_sum[None, :] - occ_sum[:, None]
    return (summed / denom).astype(jnp.bfloat16)


def solution(mesh):
    in_specs = (P("row", "col"), P("col", None), P("row"), P("row"), P(), P())
    out_specs = P("row", "col")
    return jax.shard_map(shards, mesh=mesh, in_specs=in_specs, out_specs=out_specs, check_vma=False)
```

profile of v0, /device:TPU:6, one launch (start us, length us, event | category | flops | bytes accessed | tf_op | source)
XLA Modules:
  0.0 348.0 jit_solution(5455306914043605092)
XLA Ops:
  0.0 5.2 %collective-permute-start = (bf16[2048,512]{1,0:T(8,128)(2,1)}, bf16[2048,512]{1,0:T(8,128)(2,1)S(1)}, u32[]{:S(2)}, u32[]{:S(2)}) collective-permute-start(bf16[2048,512]{1,0:T(8,128)(2,1)} %param.6), channel_id=1, source_target_pairs={{0,1},{1,2},{2,3},{3,4},{4,5},{5,6},{6,7},{7,8},{8,9},{9,10},{10,1... | collective-permute-start | bytes 6291464 | tf_op jit(solution)/shard_map/ppermute | solution.py:13
  5.2 54.8 %collective-permute-done = bf16[2048,512]{1,0:T(8,128)(2,1)S(1)} collective-permute-done((bf16[2048,512]{1,0:T(8,128)(2,1)}, bf16[2048,512]{1,0:T(8,128)(2,1)S(1)}, u32[]{:S(2)}, u32[]{:S(2)}) %collective-permute-start) | collective-permute-done | bytes 2097184 | tf_op jit(solution)/shard_map/ppermute | solution.py:13
  60.0 1.9 collective-permute-start.2
  61.9 1.5 slice.35
  63.4 1.9 collective-permute-start.1
  65.3 48.7 %collective-permute-done.2 = bf16[2048,512]{1,0:T(8,128)(2,1)S(1)} collective-permute-done((bf16[2048,512]{1,0:T(8,128)(2,1)S(1)}, bf16[2048,512]{1,0:T(8,128)(2,1)S(1)}, u32[]{:S(2)}, u32[]{:S(2)}) %collective-permute-start.2) | collective-permute-done | bytes 2097184 | tf_op jit(solution)/shard_map/ppermute | solution.py:13
  114.0 1.9 collective-permute-start.4
  116.0 31.8 %collective-permute-done.1 = bf16[512,1536]{1,0:T(8,128)(2,1)S(1)} collective-permute-done((bf16[512,1536]{1,0:T(8,128)(2,1)S(1)}, bf16[512,1536]{1,0:T(8,128)(2,1)S(1)}, u32[]{:S(2)}, u32[]{:S(2)}) %collective-permute-start.1) | collective-permute-done | bytes 1572896 | tf_op jit(solution)/shard_map/ppermute | solution.py:13
  147.9 1.9 collective-permute-start.3
  149.8 2.3 fusion.7
  152.1 61.3 %collective-permute-done.3 = bf16[512,1024]{1,0:T(8,128)(2,1)S(1)} collective-permute-done((bf16[512,1024]{1,0:T(8,128)(2,1)S(1)}, bf16[512,1024]{1,0:T(8,128)(2,1)S(1)}, u32[]{:S(2)}, u32[]{:S(2)}) %collective-permute-start.3) | collective-permute-done | bytes 1048608 | tf_op jit(solution)/shard_map/ppermute | solution.py:13
  213.5 1.9 collective-permute-start.5
  215.4 1.3 fusion.5
  216.6 1.3 fusion.3
  217.9 13.2 %collective-permute-done.5 = bf16[512,512]{1,0:T(8,128)(2,1)S(1)} collective-permute-done((bf16[512,512]{1,0:T(8,128)(2,1)S(1)}, bf16[512,512]{1,0:T(8,128)(2,1)S(1)}, u32[]{:S(2)}, u32[]{:S(2)}) %collective-permute-start.5) | collective-permute-done | bytes 524320 | tf_op jit(solution)/shard_map/ppermute | solution.py:13
  231.2 3.5 add_add_fusion
  234.6 2.6 collective-permute-start.6
  237.3 0.6 select_reduce_fusion.2
  237.9 0.9 select_reduce_fusion
  238.9 87.9 %collective-permute-done.6 = f32[2048,512]{1,0:T(8,128)} collective-permute-done((f32[2048,512]{1,0:T(8,128)}, f32[2048,512]{1,0:T(8,128)}, u32[]{:S(2)}, u32[]{:S(2)}) %collective-permute-start.6) | collective-permute-done | bytes 4194336 | tf_op jit(solution)/shard_map/ppermute | solution.py:17
  326.7 11.7 %gather_fusion = f32[2048,512]{1,0:T(8,128)} fusion(f32[2048,512]{1,0:T(8,128)} %collective-permute-done.6, s32[2048]{0:T(1024)S(1)} %broadcast_clamp_fusion), kind=kCustom, calls=%fused_computation | custom fusion | bytes 8396800 | tf_op jit(solution)/shard_map/jit(_take)/gather | solution.py:51
  338.5 2.5 broadcast_select_fusion
  341.0 1.5 fusion.19
  342.8 5.1 %fusion.2 = bf16[2048,512]{1,0:T(8,128)(2,1)} fusion(f32[2048,512]{1,0:T(8,128)} %add_add_fusion, f32[2048,511]{1,0:T(8,128)S(1)} %get-tuple-element.10, f32[2048,1]{1,0:T(8,128)S(1)} %get-tuple-element.12, f32[2048,1]{1,0:T(8,128)S(1)} %get-tuple-element.11, f32[2048,511]{1,0:T(8,128)S(1)} %get-tuple-element.9, f32[2048]{0:T(1024)S(1)} %add.99, ...), kind=kLoop, calls=%fused_computation.5 | loop fusion | flops 7340032 | bytes 14690816 | tf_op jit(solution)/shard_map/convert_element_type | solution.py:60
  (21 shorter events, 0.7 us)
Async XLA Ops:
  0.0 149.8 %copy-start = (bf16[2048,512]{1,0:T(8,128)(2,1)S(1)}, bf16[2048,512]{1,0:T(8,128)(2,1)}, u32[]{:S(2)}) copy-start(bf16[2048,512]{1,0:T(8,128)(2,1)} %param.6) | copy-start | bytes 6291460
  0.0 60.0 %collective-permute-start = (bf16[2048,512]{1,0:T(8,128)(2,1)}, bf16[2048,512]{1,0:T(8,128)(2,1)S(1)}, u32[]{:S(2)}, u32[]{:S(2)}) collective-permute-start(bf16[2048,512]{1,0:T(8,128)(2,1)} %param.6), channel_id=1, source_target_pairs={{0,1},{1,2},{2,3},{3,4},{4,5},{5,6},{6,7},{7,8},{8,9},{9,10},{10,1... | collective-permute-start | bytes 6291464 | tf_op jit(solution)/shard_map/ppermute | solution.py:13
  60.0 54.1 %collective-permute-start.2 = (bf16[2048,512]{1,0:T(8,128)(2,1)S(1)}, bf16[2048,512]{1,0:T(8,128)(2,1)S(1)}, u32[]{:S(2)}, u32[]{:S(2)}) collective-permute-start(bf16[2048,512]{1,0:T(8,128)(2,1)S(1)} %collective-permute-done), channel_id=1, source_target_pairs={{0,1},{1,2},{2,3},{3,4},{4,5},{5,6},{6,7},{7,8},{8,9},{9,10},{10,1... | collective-permute-start | bytes 6291464 | tf_op jit(solution)/shard_map/ppermute | solution.py:13
  63.4 84.3 %collective-permute-start.1 = (bf16[512,1536]{1,0:T(8,128)(2,1)S(1)}, bf16[512,1536]{1,0:T(8,128)(2,1)S(1)}, u32[]{:S(2)}, u32[]{:S(2)}) collective-permute-start(bf16[512,1536]{1,0:T(8,128)(2,1)S(1)} %slice.35), channel_id=1, source_target_pairs={{0,1},{1,2},{2,3},{3,4},{4,5},{5,6},{6,7},{7,8},{8,9},{9,10},{10,1... | collective-permute-start | bytes 4718600 | tf_op jit(solution)/shard_map/ppermute | solution.py:13
  114.0 117.1 %collective-permute-start.4 = (bf16[2048,512]{1,0:T(8,128)(2,1)S(1)}, bf16[2048,512]{1,0:T(8,128)(2,1)S(1)}, u32[]{:S(2)}, u32[]{:S(2)}) collective-permute-start(bf16[2048,512]{1,0:T(8,128)(2,1)S(1)} %collective-permute-done.2), channel_id=1, source_target_pairs={{0,1},{1,2},{2,3},{3,4},{4,5},{5,6},{6,7},{7,8},{8,9},{9,10},{10,1... | collective-permute-start | bytes 6291464 | tf_op jit(solution)/shard_map/ppermute | solution.py:13
  147.9 65.5 %collective-permute-start.3 = (bf16[512,1024]{1,0:T(8,128)(2,1)S(1)}, bf16[512,1024]{1,0:T(8,128)(2,1)S(1)}, u32[]{:S(2)}, u32[]{:S(2)}) collective-permute-start(bf16[512,1024]{1,0:T(8,128)(2,1)S(1)} %slice.47), channel_id=1, source_target_pairs={{0,1},{1,2},{2,3},{3,4},{4,5},{5,6},{6,7},{7,8},{8,9},{9,10},{10,1... | collective-permute-start | bytes 3145736 | tf_op jit(solution)/shard_map/ppermute | solution.py:13
  213.5 17.7 %collective-permute-start.5 = (bf16[512,512]{1,0:T(8,128)(2,1)S(1)}, bf16[512,512]{1,0:T(8,128)(2,1)S(1)}, u32[]{:S(2)}, u32[]{:S(2)}) collective-permute-start(bf16[512,512]{1,0:T(8,128)(2,1)S(1)} %slice.49), channel_id=1, source_target_pairs={{0,1},{1,2},{2,3},{3,4},{4,5},{5,6},{6,7},{7,8},{8,9},{9,10},{10,1... | collective-permute-start | bytes 1572872 | tf_op jit(solution)/shard_map/ppermute | solution.py:13
  217.9 19.3 %copy-start.2 = (s32[2048]{0:T(1024)S(1)}, s32[2048]{0:T(1024)}, u32[]{:S(2)}) copy-start(s32[2048]{0:T(1024)} %param.8) | copy-start | bytes 24580
  217.9 19.3 %copy-start.3 = (f32[200]{0:T(256)S(1)}, f32[200]{0:T(256)}, u32[]{:S(2)}) copy-start(f32[200]{0:T(256)} %param.10) | copy-start | bytes 2404
  217.9 19.9 %copy-start.4 = (f32[2000]{0:T(1024)S(1)}, f32[2000]{0:T(1024)}, u32[]{:S(2)}) copy-start(f32[2000]{0:T(1024)} %param.11) | copy-start | bytes 24004
  217.9 20.9 %copy-start.1 = (s32[2048]{0:T(1024)S(1)}, s32[2048]{0:T(1024)}, u32[]{:S(2)}) copy-start(s32[2048]{0:T(1024)} %param.9) | copy-start | bytes 24580
  234.6 92.1 %collective-permute-start.6 = (f32[2048,512]{1,0:T(8,128)}, f32[2048,512]{1,0:T(8,128)}, u32[]{:S(2)}, u32[]{:S(2)}) collective-permute-start(f32[2048,512]{1,0:T(8,128)} %add_add_fusion), channel_id=1, source_target_pairs={{0,256},{32,288},{64,320},{96,352},{128,384},{160,416},{192,448},{... | collective-permute-start | bytes 12582920 | tf_op jit(solution)/shard_map/ppermute | solution.py:17
where the time goes:
time: 348 us
  waiting for transfers between devices  298 us (86%)
  starting transfers between devices  17.4 us (5%)
  local copies, waits for them, and re-layouts  15.3 us (4%)
  other arithmetic  9.18 us (3%)
  matrix products  8.26 us (2%)
    ppermute x6, waiting for transfers between devices, passed_along(): return lax.ppermute(value, axis, pairs)  210 us
    ppermute x1, waiting for transfers between devices, partner_2(): lax.ppermute(x, axis, [(i, i ^ 1 << apart) for i in range(lax.axis_size(a...  87.9 us
    ppermute x6, starting transfers between devices, passed_along(): return lax.ppermute(value, axis, pairs)  14.8 us
    gather x1, local copies, waits for them, and re-layouts, shards(): opposite = jnp.take(partner_sums, local_partner, axis=0)  11.7 us
  transfers between devices with their start and end apart: 7, of which 6 were waited for; matrix products, arithmetic and copies ran while one was open for 2% of the time, Pallas kernels for 0%

commit v1 on v0

v1 whole, which is shorter than its diff:
```python
import functools

import jax
import jax.numpy as jnp
from jax import lax
from jax.experimental import pallas as pl
from jax.experimental.pallas import tpu as pltpu
from jax.sharding import PartitionSpec as P

NOCC = 200
NV = 2000
STOPS = 4
CHUNK = 128
LEVELS = 32767.0
MESH = pl.DeviceIdType.MESH


def table_lookup(table, positions):
    slots = jnp.arange(table.shape[0], dtype=jnp.int32)
    return jnp.sum(jnp.where(positions[:, None] == slots[None, :], table[None, :], 0.0), axis=1)


def encode(values, code_ref, scale_ref):
    top = jnp.maximum(jnp.max(jnp.abs(values), axis=0, keepdims=True), 1e-30)
    code = jnp.round(values * (LEVELS / top))
    code_ref[...] = code.astype(jnp.int32).astype(jnp.int16)
    scale_ref[...] = top * (1.0 / LEVELS)


def decode(code_ref, scale_ref):
    return code_ref[...].astype(jnp.int32).astype(jnp.float32) * scale_ref[...]


def kernel(
    chunks,
    width,
    row_half,
    col_count,
    amp,
    integ,
    slot_row,
    slot_col,
    occ_row,
    vir_row,
    out,
    weights,
    rows_send,
    rows_recv,
    part0,
    part1,
    part2,
    occ_chunk,
    code_send,
    code_recv,
    scale_send,
    scale_recv,
    inc_send,
    inc_all,
    rows_ssem,
    rows_rsem,
    code_ssem,
    code_rsem,
    scale_ssem,
    scale_rsem,
    inc_ssem,
    inc_rsem,
):
    row = lax.axis_index("row")
    col = lax.axis_index("col")
    upper = row // row_half
    odd = col % 2
    mine = (upper + odd) % 2
    half = chunks * CHUNK
    row_count = 2 * half
    partner = (row + row_half) % (2 * row_half)
    col_up = (col + 2) % col_count
    col_down = (col + col_count - 2) % col_count
    col_flip = col + 1 - 2 * odd

    barrier = pltpu.get_barrier_semaphore()
    for peer in ((partner, col), (partner, col_flip), (row, col_up), (row, col_down)):
        pl.semaphore_signal(barrier, inc=1, device_id=peer, device_id_type=MESH)

    def send_rows(c):
        return pltpu.make_async_remote_copy(
            src_ref=rows_send.at[c],
            dst_ref=rows_recv.at[c],
            send_sem=rows_ssem.at[c],
            recv_sem=rows_rsem.at[c],
            device_id=(partner, col),
            device_id_type=MESH,
        )

    def send_code(stream, c):
        peer = ((row, col_up), (partner, col_flip), (row, col_up))[stream]
        data = pltpu.make_async_remote_copy(
            src_ref=code_send.at[stream, c],
            dst_ref=code_recv.at[stream, c],
            send_sem=code_ssem.at[stream, c],
            recv_sem=code_rsem.at[stream, c],
            device_id=peer,
            device_id_type=MESH,
        )
        scale = pltpu.make_async_remote_copy(
            src_ref=scale_send.at[stream, c],
            dst_ref=scale_recv.at[stream, c],
            send_sem=scale_ssem.at[stream, c],
            recv_sem=scale_rsem.at[stream, c],
            device_id=peer,
            device_id_type=MESH,
        )
        return data, scale

    def send_inc(c):
        return pltpu.make_async_remote_copy(
            src_ref=inc_send.at[c],
            dst_ref=inc_all.at[c, pl.ds(CHUNK, CHUNK)],
            send_sem=inc_ssem.at[c],
            recv_sem=inc_rsem.at[c],
            device_id=(partner, col),
            device_id_type=MESH,
        )

    def push(stream, c, values):
        encode(values, code_send.at[stream, c], scale_send.at[stream, c])
        for copy in send_code(stream, c):
            copy.start()

    def arrived(stream, c):
        for copy in send_code(stream, c):
            copy.wait_recv()
        return decode(code_recv.at[stream, c], scale_recv.at[stream, c])

    def picks(base):
        places = base + lax.broadcasted_iota(jnp.int32, (CHUNK, row_count), 0)
        return slot_row[...] == places

    def own_rows(choice):
        one_hot = jnp.where(choice, 1.0, 0.0).astype(jnp.bfloat16)
        return jnp.dot(one_hot, amp[...], preferred_element_type=jnp.float32).astype(jnp.bfloat16)

    rows_send[0] = own_rows(picks((1 - mine) * half))
    pl.semaphore_wait(barrier, 4)
    send_rows(0).start()

    @pl.loop(1, chunks)
    def _(c):
        rows_send[c] = own_rows(picks((1 - mine) * half + c * CHUNK))
        send_rows(c).start()

    out[...] = jnp.zeros_like(out)
    tile = 256
    left = lax.broadcasted_iota(jnp.int32, (tile, tile), 0)
    right = lax.broadcasted_iota(jnp.int32, (tile, tile), 1)
    step = 1 - 2 * (right % 2)
    for side in range(2):
        moved = upper if side == 0 else 1 - upper
        swap = jnp.where(left == right + moved * step, 1.0, 0.0).astype(jnp.bfloat16)
        for t in range(STOPS * width // tile):
            cols = pl.ds(t * tile, tile)
            weights[side, :, cols] = jnp.dot(
                integ[:, cols], swap, preferred_element_type=jnp.float32
            ).astype(jnp.bfloat16)

    even_lane = lax.broadcasted_iota(jnp.int32, (CHUNK, width), 1) % 2 == 0
    lanes = lax.broadcasted_iota(jnp.int32, (row_count, CHUNK), 1)
    is_even = (1 - odd).astype(jnp.float32)
    is_odd = odd.astype(jnp.float32)
    is_upper = lax.broadcasted_iota(jnp.int32, (CHUNK, width), 1) * 0 + upper > 0

    @pl.loop(0, chunks + 4)
    def _(t):
        @pl.when(t < chunks)
        def _():
            choice = picks(mine * half + t * CHUNK)
            occ_chunk[t] = jnp.sum(jnp.where(choice, occ_row[...], 0.0), axis=1, keepdims=True)
            own = own_rows(choice)
            send_rows(t).wait_recv()
            other = rows_recv[t]

            def product(s):
                cols = pl.ds(s * width, width)
                return jnp.dot(own, weights[0, :, cols], preferred_element_type=jnp.float32) + jnp.dot(
                    other, weights[1, :, cols], preferred_element_type=jnp.float32
                )

            push(0, t, product(3))
            part1[t] = product(1)
            part2[t] = product(2)
            part0[t] = product(0)

        @pl.when((t >= 1) & (t < chunks + 1))
        def _():
            c = t - 1
            push(1, c, part1[c] + arrived(0, c))

        @pl.when((t >= 2) & (t < chunks + 2))
        def _():
            c = t - 2
            across = arrived(1, c)
            push(2, c, part2[c] + across * is_even)
            part0[c] = part0[c] + across * is_odd

        @pl.when((t >= 3) & (t < chunks + 3))
        def _():
            c = t - 3
            total = part0[c] + arrived(2, c)
            plain = total / (vir_row[...] - occ_chunk[c])
            mirrored = jnp.where(
                even_lane,
                pltpu.roll(plain, width - 1, axis=1),
                pltpu.roll(plain, 1, axis=1),
            )
            inc_send[c] = jnp.where(is_upper, plain, mirrored).astype(jnp.bfloat16)
            send_inc(c).start()
            inc_all[c, pl.ds(0, CHUNK)] = jnp.where(is_upper, mirrored, plain).astype(jnp.bfloat16)

        @pl.when(t >= 4)
        def _():
            c = t - 4
            send_inc(c).wait_recv()
            values = inc_all[c]
            group = min(512, row_count)
            for j in range(row_count // group):
                rows = pl.ds(j * group, group)
                at = slot_col[rows, :]
                lane = lanes[j * group : (j + 1) * group]
                near = jnp.where(at == lane + (mine * half + c * CHUNK), 1.0, 0.0)
                far = jnp.where(at == lane + ((1 - mine) * half + c * CHUNK), 1.0, 0.0)
                one_hot = jnp.concatenate([near, far], axis=1).astype(jnp.bfloat16)
                found = jnp.dot(one_hot, values, preferred_element_type=jnp.float32)
                out[rows, :] = out[rows, :] + found.astype(jnp.bfloat16)

    @pl.loop(0, chunks)
    def _(c):
        send_rows(c).wait_send()
        for stream in range(3):
            for copy in send_code(stream, c):
                copy.wait_send()
        send_inc(c).wait_send()


def shards(amplitudes, integrals, pair_index, partner, occ_energy, vir_energy):
    row_count, width = amplitudes.shape
    row_half = lax.axis_size("row") // 2
    col_count = lax.axis_size("col")
    chunks = row_count // 2 // CHUNK
    upper = lax.axis_index("row") // row_half
    own_place = jnp.arange(row_count, dtype=jnp.int32)
    slot = jnp.where(upper == 0, own_place, partner % row_count)
    occ_sum = table_lookup(occ_energy, pair_index // NOCC) + table_lookup(
        occ_energy, pair_index % NOCC
    )
    global_pair = lax.axis_index("col") * width + jnp.arange(width, dtype=jnp.int32)
    unordered = global_pair // 2
    vir_sum = table_lookup(vir_energy, unordered // NV) + table_lookup(vir_energy, unordered % NV)
    vmem = pl.BlockSpec(memory_space=pltpu.VMEM)
    dma = pltpu.SemaphoreType.DMA
    return pl.pallas_call(
        functools.partial(kernel, chunks, width, row_half, col_count),
        out_shape=jax.ShapeDtypeStruct((row_count, width), jnp.bfloat16),
        in_specs=[vmem] * 6,
        out_specs=vmem,
        scratch_shapes=[
            pltpu.VMEM((2, width, STOPS * width), jnp.bfloat16),
            pltpu.VMEM((chunks, CHUNK, width), jnp.bfloat16),
            pltpu.VMEM((chunks, CHUNK, width), jnp.bfloat16),
            pltpu.VMEM((chunks, CHUNK, width), jnp.float32),
            pltpu.VMEM((chunks, CHUNK, width), jnp.float32),
            pltpu.VMEM((chunks, CHUNK, width), jnp.float32),
            pltpu.VMEM((chunks, CHUNK, 1), jnp.float32),
            pltpu.VMEM((3, chunks, CHUNK, width), jnp.int16),
            pltpu.VMEM((3, chunks, CHUNK, width), jnp.int16),
            pltpu.VMEM((3, chunks, 1, width), jnp.float32),
            pltpu.VMEM((3, chunks, 1, width), jnp.float32),
            pltpu.VMEM((chunks, CHUNK, width), jnp.bfloat16),
            pltpu.VMEM((chunks, 2 * CHUNK, width), jnp.bfloat16),
            dma((chunks,)),
            dma((chunks,)),
            dma((3, chunks)),
            dma((3, chunks)),
            dma((3, chunks)),
            dma((3, chunks)),
            dma((chunks,)),
            dma((chunks,)),
        ],
        compiler_params=pltpu.CompilerParams(
            collective_id=0, has_side_effects=True, vmem_limit_bytes=56 * 1024 * 1024
        ),
    )(
        amplitudes,
        integrals,
        slot[None, :],
        jnp.broadcast_to(slot[:, None], (row_count, CHUNK)),
        occ_sum[None, :],
        vir_sum[None, :],
    )


def solution(mesh):
    in_specs = (P("row", "col"), P("col", None), P("row"), P("row"), P(), P())
    out_specs = P("row", "col")
    return jax.shard_map(shards, mesh=mesh, in_specs=in_specs, out_specs=out_specs, check_vma=False)
```

time: 348 us -> 86.9 us (0.25)
  waiting for transfers between devices: 298 us -> 0 us
  Pallas kernels: 0 us -> 76.1 us
  starting transfers between devices: 17.4 us -> 0 us
  local copies, waits for them, and re-layouts: 15.3 us -> 4.35 us
  matrix products: 8.26 us -> 0 us
  other arithmetic: 9.18 us -> 5.51 us
    ppermute x7 -> x0, waiting for transfers between devices: 298 us -> none  [the longest x6 210 us: passed_along(): return lax.ppermute(value, axis, pairs)]
    pallas_call x0 -> x1, Pallas kernels: none -> 76.1 us  [shards(): pl.pallas_call(functools.partial(kernel, chunks, width, row_half, col_cou...]
    ppermute x7 -> x0, starting transfers between devices: 17.4 us -> none  [the longest x6 14.8 us: passed_along(): return lax.ppermute(value, axis, pairs)]
    gather x1 -> x0, local copies, waits for them, and re-layouts: 11.7 us -> none  [shards(): opposite = jnp.take(partner_sums, local_partner, axis=0)]
    dot_general x4 -> x0, matrix products: 8.26 us -> none  [the longest x3 5.97 us: contract_stops(): jnp.dot(moving, slab_rest[:, :pair_width], preferred_element_type=jnp.flo...]
    convert_element_type x1 -> x0, other arithmetic: 5.14 us -> none  [shards(): return (summed / denom).astype(jnp.bfloat16)]
    slice x5 -> x0, local copies, waits for them, and re-layouts: 3.53 us -> none  [the longest x2 1.85 us: mirror_pairs(): jnp.roll(values, -1, axis=1)]
  transfers between devices with their start and end apart: 7 -> 0, of which waited for: 6 -> 0; matrix products, arithmetic and copies ran while one was open for 2% -> 0% of each run, Pallas kernels for 0% -> 0%
where the time goes in v1:
time: 86.9 us; the launch traced here: 86 us
  Pallas kernels  76.1 us (88%)
  other arithmetic  5.51 us (6%)
  local copies, waits for them, and re-layouts  4.35 us (5%)
    pallas_call x1, Pallas kernels, shards(): pl.pallas_call(functools.partial(kernel, chunks, width, row_half, col_cou...  76.1 us
    unnamed x3, local copies, waits for them, and re-layouts  3.05 us
    reduce_sum x2, other arithmetic, table_lookup(): jnp.sum(jnp.where(positions[:, None] == slots[None, :], table[None, :], 0...  2.87 us

profile of v1, /device:TPU:6, one launch (start us, length us, event | category | flops | bytes accessed | tf_op | source)
XLA Modules:
  0.0 86.0 jit_solution(17107658089309177347)
XLA Ops:
  0.0 1.6 %select_reduce_fusion = (f32[512]{0:T(512)S(1)}, f32[512]{0:T(512)S(1)}) fusion(s32[512]{0:T(512)S(1)} %get-tuple-element.11, f32[2000]{0:T(1024)} %param.11, s32[512]{0:T(512)S(1)} %get-tuple-element.12), kind=kLoop, calls=%fused_computation | loop fusion | flops 6142976 | bytes 16192 | tf_op jit(solution)/shard_map/reduce_sum | solution.py:20
  1.7 0.6 add.81
  2.3 0.7 fusion.1
  3.0 0.0 copy-start
  3.0 0.7 add_select_fusion.1
  3.7 1.2 %select_reduce_fusion.2 = (f32[2048]{0:T(1024)S(1)}, f32[2048]{0:T(1024)S(1)}) fusion(s32[2048]{0:T(1024)S(1)} %get-tuple-element.10, f32[200]{0:T(256)} %param.10, s32[2048]{0:T(1024)S(1)} %get-tuple-element.9), kind=kLoop, calls=%fused_computation.4 | loop fusion | flops 2453504 | bytes 33568 | tf_op jit(solution)/shard_map/reduce_sum | solution.py:20
  4.9 0.6 add.76
  5.5 1.3 %broadcast_in_dim.56.slot_col = s32[2048,128]{1,0:T(8,128)} broadcast(s32[2048]{0:T(1024)S(1)} %fusion.1), dimensions={0} | broadcast | bytes 1056768 | tf_op jit(solution)/shard_map/broadcast_in_dim | solution.py:294
  6.8 0.0 copy-done
  6.8 76.1 %shard_map.64 = bf16[2048,512]{1,0:T(8,128)(2,1)} custom-call(bf16[2048,512]{1,0:T(8,128)(2,1)} %amp.1, bf16[512,2048]{1,0:T(8,128)(2,1)} %integ.1, s32[1,2048]{1,0:T(1,128)} %bitcast.3, s32[2048,128]{1,0:T(8,128)} %broadcast_in_dim.56.slot_col, f32[1,2048]{1,0:T(1,128)} %bitcast.4, f32[1,512]{1,0:T(1,128)} %bitcast.5), custom_call_target="tpu_custom_call" | custom-call | tf_op jit(solution)/shard_map/pallas_call | solution.py:259
  82.9 3.0 %copy.8 = bf16[2048,512]{1,0:T(8,128)(2,1)} copy(bf16[2048,512]{1,0:T(8,128)(2,1)} %shard_map.64) | data formatting | bytes 4194304
  (1 shorter events, 0.0 us)
Async XLA Ops:
  3.0 3.9 %copy-start = (s32[2048]{0:T(1024)}, s32[2048]{0:T(1024)S(1)}, u32[]{:S(2)}) copy-start(s32[2048]{0:T(1024)S(1)} %fusion.1) | copy-start | bytes 24580

commit v2 on v1

v2 whole, which is shorter than its diff:
```python
import functools

import jax
import jax.numpy as jnp
from jax import lax
from jax.experimental import pallas as pl
from jax.experimental.pallas import tpu as pltpu
from jax.sharding import PartitionSpec as P

NOCC = 200
NV = 2000
STOPS = 4
CHUNK = 128
LAGS = (2, 4, 6, 8)
ZA, YA, ZB, YB = range(4)
LEVELS = 32767.0
MESH = pl.DeviceIdType.MESH
F32 = jnp.float32
BF16 = jnp.bfloat16


def iota(shape, dim):
    return lax.broadcasted_iota(jnp.int32, shape, dim)


def encode(values, code_ref, scale_ref):
    top = jnp.maximum(jnp.max(jnp.abs(values), axis=0, keepdims=True), 1e-30)
    code = jnp.round(values * (LEVELS / top))
    code_ref[...] = code.astype(jnp.int32).astype(jnp.int16)
    scale_ref[...] = top * (1.0 / LEVELS)


def decode(code_ref, scale_ref):
    return code_ref[...].astype(jnp.int32).astype(F32) * scale_ref[...]


def lookup(table, position):
    slots = iota((position.shape[0], table.shape[1]), 1).astype(F32)
    return jnp.sum(jnp.where(slots == position, table, 0.0), axis=1, keepdims=True)


def pair_sum(table, base, position):
    first = jnp.floor((position + 0.5) * (1.0 / base))
    return lookup(table, first) + lookup(table, position - first * base)


def place(slot_ref, inc, first, rows):
    at = slot_ref[rows, :]
    lane = iota(at.shape, 1)
    near = jnp.where(at == lane + first[0], 1.0, 0.0)
    far = jnp.where(at == lane + first[1], 1.0, 0.0)
    one_hot = jnp.concatenate([near, far], axis=1).astype(BF16)
    return jnp.dot(one_hot, inc, preferred_element_type=F32).astype(BF16)


def kernel(
    chunks,
    width,
    row_half,
    col_count,
    amp_hbm,
    integ_hbm,
    partner_hbm,
    pair_hbm,
    occ_hbm,
    vir_hbm,
    acc,
    slot_col,
    partner_row,
    pair_row,
    occ_table,
    vir_table,
    amp,
    integ,
    mirror,
    slot_row,
    pair_f,
    vir_row,
    rows_send,
    rows_all,
    part,
    total,
    occ_chunk,
    code_send,
    code_recv,
    scale_send,
    scale_recv,
    inc_send,
    inc_all,
    load_sem,
    rows_ssem,
    rows_rsem,
    code_ssem,
    code_rsem,
    scale_ssem,
    scale_rsem,
    inc_ssem,
    inc_rsem,
):
    row = lax.axis_index("row")
    col = lax.axis_index("col")
    upper = row // row_half
    odd = col % 2
    mine = (upper + odd) % 2
    half = chunks * CHUNK
    row_count = 2 * half
    partner = (row + row_half) % (2 * row_half)
    col_up = (col + 2) % col_count
    col_down = (col + col_count - 2) % col_count
    col_flip = col + 1 - 2 * odd

    loads = [
        pltpu.make_async_copy(source, target, load_sem.at[i])
        for i, (source, target) in enumerate(
            (
                (partner_hbm, partner_row),
                (amp_hbm, amp),
                (pair_hbm, pair_row),
                (occ_hbm, occ_table),
                (vir_hbm, vir_table),
                (integ_hbm, integ),
            )
        )
    ]
    for load in loads[:-1]:
        load.start()

    barrier = pltpu.get_barrier_semaphore()
    for peer in ((partner, col), (partner, col_flip), (row, col_up), (row, col_down)):
        pl.semaphore_signal(barrier, inc=1, device_id=peer, device_id_type=MESH)

    def send_rows(c, slot):
        return pltpu.make_async_remote_copy(
            src_ref=rows_send.at[c],
            dst_ref=rows_all.at[slot, c],
            send_sem=rows_ssem.at[c],
            recv_sem=rows_rsem.at[c],
            device_id=(partner, col),
            device_id_type=MESH,
        )

    def send_code(stream, c):
        peer = (row, col_up) if stream in (ZA, ZB) else (partner, col_flip)
        data = pltpu.make_async_remote_copy(
            src_ref=code_send.at[stream, c],
            dst_ref=code_recv.at[stream, c],
            send_sem=code_ssem.at[stream, c],
            recv_sem=code_rsem.at[stream, c],
            device_id=peer,
            device_id_type=MESH,
        )
        scale = pltpu.make_async_remote_copy(
            src_ref=scale_send.at[stream, c],
            dst_ref=scale_recv.at[stream, c],
            send_sem=scale_ssem.at[stream, c],
            recv_sem=scale_rsem.at[stream, c],
            device_id=peer,
            device_id_type=MESH,
        )
        return data, scale

    def send_inc(c):
        return pltpu.make_async_remote_copy(
            src_ref=inc_send.at[c],
            dst_ref=inc_all.at[c, pl.ds(CHUNK, CHUNK)],
            send_sem=inc_ssem.at[c],
            recv_sem=inc_rsem.at[c],
            device_id=(partner, col),
            device_id_type=MESH,
        )

    def push(stream, c, values):
        encode(values, code_send.at[stream, c], scale_send.at[stream, c])
        for copy in send_code(stream, c):
            copy.start()

    def arrived(stream, c):
        for copy in send_code(stream, c):
            copy.wait_recv()
        return decode(code_recv.at[stream, c], scale_recv.at[stream, c])

    def picks(base):
        return slot_row[...] == base + iota((CHUNK, row_count), 0)

    def own_rows(choice):
        one_hot = jnp.where(choice, 1.0, 0.0).astype(BF16)
        return jnp.dot(one_hot, amp[...], preferred_element_type=F32).astype(BF16)

    loads[0].wait()
    slot_row[...] = jnp.where(
        iota((1, row_count), 1) * 0 + upper > 0,
        partner_row[...] - partner * row_count,
        iota((1, row_count), 1),
    )
    loads[1].wait()
    loads[-1].start()
    rows_send[0] = own_rows(picks((1 - mine) * half))
    pl.semaphore_wait(barrier, 4)
    send_rows(0, upper).start()

    @pl.loop(1, chunks)
    def _(c):
        rows_send[c] = own_rows(picks((1 - mine) * half + c * CHUNK))
        send_rows(c, upper).start()

    for load in loads[2:]:
        load.wait()
    tile = 256
    right = iota((tile, tile), 1)
    swap = jnp.where(iota((tile, tile), 0) == right + 1 - 2 * (right % 2), 1.0, 0.0).astype(BF16)
    for t in range(STOPS * width // tile):
        cols = pl.ds(t * tile, tile)
        mirror[:, cols] = jnp.dot(integ[:, cols], swap, preferred_element_type=F32).astype(BF16)
    pair_f[...] = pair_row[...].astype(F32)

    even_lane = iota((CHUNK, width), 1) % 2 == 0
    is_even = odd == 0
    is_odd = odd == 1
    is_upper = iota((CHUNK, width), 1) * 0 + upper > 0

    def first_hop(c):
        choice = picks(mine * half + c * CHUNK)
        rows_all[upper, c] = own_rows(choice)
        send_rows(c, 1 - upper).wait_recv()
        low = rows_all[0, c]
        high = rows_all[1, c]

        def product(s):
            cols = pl.ds(s * width, width)
            return jnp.dot(low, integ[:, cols], preferred_element_type=F32) + jnp.dot(
                high, mirror[:, cols], preferred_element_type=F32
            )

        for s in range(STOPS):
            part[s, c] = product(s)
        pair = jnp.sum(jnp.where(choice, pair_f[...], 0.0), axis=1, keepdims=True)
        occ_chunk[c] = pair_sum(occ_table[...], NOCC, pair)
        first_kind = c % 2 == 0

        @pl.when(is_odd)
        def _():
            push(ZA, c, part[3, c])

        @pl.when(is_odd & ~first_kind)
        def _():
            push(YB, c, part[2, c])

        @pl.when(is_even & first_kind)
        def _():
            push(YA, c, part[3, c])
            push(YB, c, part[1, c])

    def second_hop(c):
        first_kind = c % 2 == 0

        @pl.when(is_odd)
        def _():
            push(YA, c, part[1, c] + arrived(ZA, c))

        @pl.when(is_odd & first_kind)
        def _():
            push(ZB, c, part[2, c] + arrived(YA, c))

        @pl.when(is_even & ~first_kind)
        def _():
            push(ZB, c, part[3, c] + arrived(YB, c))

    def third_hop(c):
        first_kind = c % 2 == 0

        @pl.when(is_even & ~first_kind)
        def _():
            push(YA, c, part[1, c] + arrived(ZB, c))

        @pl.when(is_even)
        def _():
            push(ZA, c, part[2, c] + arrived(YA, c))

    def finish(c):
        first_kind = c % 2 == 0

        @pl.when(is_even)
        def _():
            total[...] = part[0, c] + arrived(ZA, c)

        @pl.when(is_odd & first_kind)
        def _():
            total[...] = part[0, c] + arrived(ZB, c) + arrived(YB, c)

        @pl.when(is_odd & ~first_kind)
        def _():
            total[...] = part[0, c] + arrived(YA, c)

        plain = total[...] / (vir_row[...] - occ_chunk[c])
        mirrored = jnp.where(
            even_lane,
            pltpu.roll(plain, width - 1, axis=1),
            pltpu.roll(plain, 1, axis=1),
        )
        inc_send[c] = jnp.where(is_upper, plain, mirrored).astype(BF16)
        send_inc(c).start()
        inc_all[c, pl.ds(0, CHUNK)] = jnp.where(is_upper, mirrored, plain).astype(BF16)

    def spread(c):
        send_inc(c).wait_recv()
        values = inc_all[c]
        first = (mine * half + c * CHUNK, (1 - mine) * half + c * CHUNK)
        group = min(512, row_count)
        for j in range(row_count // group):
            rows = pl.ds(j * group, group)
            acc[rows, :] = acc[rows, :] + place(slot_col, values, first, rows)

    @pl.loop(0, chunks + LAGS[3])
    def _(t):
        @pl.when(t < chunks)
        def _():
            first_hop(t)

        @pl.when((t >= LAGS[0]) & (t < chunks + LAGS[0]))
        def _():
            second_hop(t - LAGS[0])

        @pl.when((t >= LAGS[1]) & (t < chunks + LAGS[1]))
        def _():
            third_hop(t - LAGS[1])

        @pl.when(t == LAGS[1])
        def _():
            pairs = width // 2
            unordered = col * pairs + iota((pairs, 1), 0)
            values = pair_sum(vir_table[...], NV, unordered.astype(F32))
            same = iota((pairs, width), 1) // 2 == iota((pairs, width), 0)
            vir_row[...] = jnp.sum(jnp.where(same, values, 0.0), axis=0, keepdims=True)
            for j in range(row_count // CHUNK):
                rows = pl.ds(j * CHUNK, CHUNK)
                block = jnp.broadcast_to(slot_row[:, rows], (CHUNK, CHUNK))
                slot_col[rows, :] = block.T
            acc[...] = jnp.zeros_like(acc)

        @pl.when((t >= LAGS[2]) & (t < chunks + LAGS[2]))
        def _():
            finish(t - LAGS[2])

        @pl.when(t >= LAGS[3])
        def _():
            spread(t - LAGS[3])

    @pl.loop(0, chunks)
    def _(c):
        first_kind = c % 2 == 0
        send_rows(c, upper).wait_send()
        send_inc(c).wait_send()
        for stream in (ZA, YA):
            for copy in send_code(stream, c):
                copy.wait_send()

        @pl.when(is_odd == first_kind)
        def _():
            for copy in send_code(ZB, c):
                copy.wait_send()

        @pl.when(is_even == first_kind)
        def _():
            for copy in send_code(YB, c):
                copy.wait_send()


def shards(amplitudes, integrals, pair_index, partner, occ_energy, vir_energy):
    row_count, width = amplitudes.shape
    row_half = lax.axis_size("row") // 2
    col_count = lax.axis_size("col")
    chunks = row_count // 2 // CHUNK
    dma = pltpu.SemaphoreType.DMA
    return pl.pallas_call(
        functools.partial(kernel, chunks, width, row_half, col_count),
        out_shape=jax.ShapeDtypeStruct((row_count, width), BF16),
        in_specs=[pl.BlockSpec(memory_space=pltpu.HBM)] * 6,
        out_specs=pl.BlockSpec(memory_space=pltpu.VMEM),
        scratch_shapes=[
            pltpu.VMEM((row_count, CHUNK), jnp.int32),
            pltpu.VMEM((1, row_count), jnp.int32),
            pltpu.VMEM((1, row_count), jnp.int32),
            pltpu.VMEM((1, occ_energy.shape[0]), F32),
            pltpu.VMEM((1, vir_energy.shape[0]), F32),
            pltpu.VMEM((row_count, width), BF16),
            pltpu.VMEM((width, STOPS * width), BF16),
            pltpu.VMEM((width, STOPS * width), BF16),
            pltpu.VMEM((1, row_count), jnp.int32),
            pltpu.VMEM((1, row_count), F32),
            pltpu.VMEM((1, width), F32),
            pltpu.VMEM((chunks, CHUNK, width), BF16),
            pltpu.VMEM((2, chunks, CHUNK, width), BF16),
            pltpu.VMEM((STOPS, chunks, CHUNK, width), F32),
            pltpu.VMEM((CHUNK, width), F32),
            pltpu.VMEM((chunks, CHUNK, 1), F32),
            pltpu.VMEM((4, chunks, CHUNK, width), jnp.int16),
            pltpu.VMEM((4, chunks, CHUNK, width), jnp.int16),
            pltpu.VMEM((4, chunks, 1, width), F32),
            pltpu.VMEM((4, chunks, 1, width), F32),
            pltpu.VMEM((chunks, CHUNK, width), BF16),
            pltpu.VMEM((chunks, 2 * CHUNK, width), BF16),
            dma((6,)),
            dma((chunks,)),
            dma((chunks,)),
            dma((4, chunks)),
            dma((4, chunks)),
            dma((4, chunks)),
            dma((4, chunks)),
            dma((chunks,)),
            dma((chunks,)),
        ],
        compiler_params=pltpu.CompilerParams(
            collective_id=0, has_side_effects=True, vmem_limit_bytes=48 * 1024 * 1024
        ),
    )(
        pltpu.with_memory_space_constraint(amplitudes, pltpu.HBM),
        pltpu.with_memory_space_constraint(integrals, pltpu.HBM),
        pltpu.with_memory_space_constraint(partner[None, :], pltpu.HBM),
        pltpu.with_memory_space_constraint(pair_index[None, :], pltpu.HBM),
        pltpu.with_memory_space_constraint(occ_energy[None, :], pltpu.HBM),
        pltpu.with_memory_space_constraint(vir_energy[None, :], pltpu.HBM),
    )


def solution(mesh):
    in_specs = (P("row", "col"), P("col", None), P("row"), P("row"), P(), P())
    out_specs = P("row", "col")
    return jax.shard_map(shards, mesh=mesh, in_specs=in_specs, out_specs=out_specs, check_vma=False)
```

time: 86.9 us -> 71 us (0.82)
  Pallas kernels: 76.1 us -> 69.5 us
  other arithmetic: 5.51 us -> 0 us
  local copies, waits for them, and re-layouts: 4.35 us -> 1.32 us
    pallas_call x1, Pallas kernels: 76.1 us -> 69.5 us  [shards(): pl.pallas_call(functools.partial(kernel, chunks, width, row_half, col_cou...]
    reduce_sum x2 -> x0, other arithmetic: 2.87 us -> none  [table_lookup(): jnp.sum(jnp.where(positions[:, None] == slots[None, :], table[None, :], 0...]
    unnamed x3 -> x1, local copies, waits for them, and re-layouts: 3.05 us -> 1.32 us
    select_n x3 -> x0, other arithmetic: 1.44 us -> none  [the longest x1 0.71 us: shards(): pair_index // NOCC]
    broadcast_in_dim x1 -> x0, local copies, waits for them, and re-layouts: 1.3 us -> none  [shards(): jnp.broadcast_to(slot[:, None], (row_count, CHUNK))]
    add x2 -> x0, other arithmetic: 1.2 us -> none  [the longest x1 0.6 us: shards(): table_lookup(vir_energy, unordered // NV)]
where the time goes in v2:
time: 71 us; the launch traced here: 70.9 us
  Pallas kernels  69.5 us (98%)
  local copies, waits for them, and re-layouts  1.32 us (2%)
    pallas_call x1, Pallas kernels, shards(): pl.pallas_call(functools.partial(kernel, chunks, width, row_half, col_cou...  69.5 us

profile of v2, /device:TPU:6, one launch (start us, length us, event | category | flops | bytes accessed | tf_op | source)
XLA Modules:
  0.0 70.9 jit_solution(12628687417379248196)
XLA Ops:
  0.0 69.5 %shard_map.64 = bf16[2048,512]{1,0:T(8,128)(2,1)S(1)} custom-call(bf16[2048,512]{1,0:T(8,128)(2,1)} %amp_hbm.1, bf16[512,2048]{1,0:T(8,128)(2,1)} %integ_hbm.1, s32[1,2048]{1,0:T(1,128)} %bitcast.4, s32[1,2048]{1,0:T(1,128)} %bitcast.5, f32[1,200]{1,0:T(1,128)} %bitcast.7, f32[1,2000]{1,0:T(1,128)} %bitcast.6), custom_call_target="tpu_custom_call" | custom-call | tf_op jit(solution)/shard_map/pallas_call | solution.py:374
  69.5 1.3 %copy.8 = bf16[2048,512]{1,0:T(8,128)(2,1)} copy(bf16[2048,512]{1,0:T(8,128)(2,1)S(1)} %shard_map.64) | data formatting | bytes 4194304

commit v3 on v2

--- a/solution.py
+++ b/solution.py
@@ -11,7 +11,8 @@
 NV = 2000
 STOPS = 4
 CHUNK = 128
-LAGS = (2, 4, 6, 8)
+PIECE = 64
+LAGS = (3, 6, 9, 13)
 ZA, YA, ZB, YB = range(4)
 LEVELS = 32767.0
 MESH = pl.DeviceIdType.MESH
@@ -103,6 +104,8 @@
     odd = col % 2
     mine = (upper + odd) % 2
     half = chunks * CHUNK
+    cuts = CHUNK // PIECE
+    pieces = chunks * cuts
     row_count = 2 * half
     partner = (row + row_half) % (2 * row_half)
     col_up = (col + 2) % col_count
@@ -162,7 +165,7 @@
     def send_inc(c):
         return pltpu.make_async_remote_copy(
             src_ref=inc_send.at[c],
-            dst_ref=inc_all.at[c, pl.ds(CHUNK, CHUNK)],
+            dst_ref=inc_all.at[c // cuts, pl.ds(CHUNK + c % cuts * PIECE, PIECE)],
             send_sem=inc_ssem.at[c],
             recv_sem=inc_rsem.at[c],
             device_id=(partner, col),
@@ -194,14 +197,21 @@
     )
     loads[1].wait()
     loads[-1].start()
-    rows_send[0] = own_rows(picks((1 - mine) * half))
+    def ready_rows(c):
+        found = own_rows(picks((1 - mine) * half + c * CHUNK))
+        for p in range(cuts):
+            rows_send[c * cuts + p] = found[p * PIECE : (p + 1) * PIECE]
+
+    ready_rows(0)
     pl.semaphore_wait(barrier, 4)
-    send_rows(0, upper).start()
+    for p in range(cuts):
+        send_rows(p, upper).start()
 
     @pl.loop(1, chunks)
     def _(c):
-        rows_send[c] = own_rows(picks((1 - mine) * half + c * CHUNK))
-        send_rows(c, upper).start()
+        ready_rows(c)
+        for p in range(cuts):
+            send_rows(c * cuts + p, upper).start()
 
     for load in loads[2:]:
         load.wait()
@@ -213,48 +223,67 @@
         mirror[:, cols] = jnp.dot(integ[:, cols], swap, preferred_element_type=F32).astype(BF16)
     pair_f[...] = pair_row[...].astype(F32)
 
-    even_lane = iota((CHUNK, width), 1) % 2 == 0
+    even_lane = iota((PIECE, width), 1) % 2 == 0
     is_even = odd == 0
     is_odd = odd == 1
-    is_upper = iota((CHUNK, width), 1) * 0 + upper > 0
+    is_upper = iota((PIECE, width), 1) * 0 + upper > 0
 
     def first_hop(c):
         choice = picks(mine * half + c * CHUNK)
-        rows_all[upper, c] = own_rows(choice)
-        send_rows(c, 1 - upper).wait_recv()
-        low = rows_all[0, c]
-        high = rows_all[1, c]
-
-        def product(s):
+        own = own_rows(choice)
+        for p in range(cuts):
+            rows_all[upper, c * cuts + p] = own[p * PIECE : (p + 1) * PIECE]
+        for p in range(cuts):
+            send_rows(c * cuts + p, 1 - upper).wait_recv()
+        low = rows_all[0, pl.ds(c * cuts, cuts)].reshape(CHUNK, width)
+        high = rows_all[1, pl.ds(c * cuts, cuts)].reshape(CHUNK, width)
+
+        def multiply(s):
             cols = pl.ds(s * width, width)
-            return jnp.dot(low, integ[:, cols], preferred_element_type=F32) + jnp.dot(
+            product = jnp.dot(low, integ[:, cols], preferred_element_type=F32) + jnp.dot(
                 high, mirror[:, cols], preferred_element_type=F32
             )
-
-        for s in range(STOPS):
-            part[s, c] = product(s)
+            for p in range(cuts):
+                part[s, c * cuts + p] = product[p * PIECE : (p + 1) * PIECE]
+
+        def push_parts(stream, s, start):
+            for p in range(start, cuts, 2):
+                push(stream, c * cuts + p, part[s, c * cuts + p])
+
+        multiply(3)
+
+        @pl.when(is_odd)
+        def _():
+            for p in range(cuts):
+                push(ZA, c * cuts + p, part[3, c * cuts + p])
+
+        @pl.when(is_even)
+        def _():
+            push_parts(YA, 3, 1)
+
+        multiply(1)
+
+        @pl.when(is_even)
+        def _():
+            push_parts(YB, 1, 1)
+
+        multiply(2)
+
+        @pl.when(is_odd)
+        def _():
+            push_parts(YB, 2, 0)
+
+        multiply(0)
         pair = jnp.sum(jnp.where(choice, pair_f[...], 0.0), axis=1, keepdims=True)
-        occ_chunk[c] = pair_sum(occ_table[...], NOCC, pair)
-        first_kind = c % 2 == 0
+        occ = pair_sum(occ_table[...], NOCC, pair)
+        for p in range(cuts):
+            occ_chunk[c * cuts + p] = occ[p * PIECE : (p + 1) * PIECE]
+
+    def second_hop(c):
+        first_kind = c % 2 == 1
 
         @pl.when(is_odd)
         def _():
-            push(ZA, c, part[3, c])
-
-        @pl.when(is_odd & ~first_kind)
-        def _():
-            push(YB, c, part[2, c])
-
-        @pl.when(is_even & first_kind)
-        def _():
-            push(YA, c, part[3, c])
-            push(YB, c, part[1, c])
-
-    def second_hop(c):
-        first_kind = c % 2 == 0
-
-        @pl.when(is_odd)
-        def _():
             push(YA, c, part[1, c] + arrived(ZA, c))
 
         @pl.when(is_odd & first_kind)
@@ -266,7 +295,7 @@
             push(ZB, c, part[3, c] + arrived(YB, c))
 
     def third_hop(c):
-        first_kind = c % 2 == 0
+        first_kind = c % 2 == 1
 
         @pl.when(is_even & ~first_kind)
         def _():
@@ -277,7 +306,7 @@
             push(ZA, c, part[2, c] + arrived(YA, c))
 
     def finish(c):
-        first_kind = c % 2 == 0
+        first_kind = c % 2 == 1
 
         @pl.when(is_even)
         def _():
@@ -299,10 +328,11 @@
         )
         inc_send[c] = jnp.where(is_upper, plain, mirrored).astype(BF16)
         send_inc(c).start()
-        inc_all[c, pl.ds(0, CHUNK)] = jnp.where(is_upper, mirrored, plain).astype(BF16)
+        inc_all[c // cuts, pl.ds(c % cuts * PIECE, PIECE)] = jnp.where(is_upper, mirrored, plain).astype(BF16)
 
     def spread(c):
-        send_inc(c).wait_recv()
+        for p in range(cuts):
+            send_inc(c * cuts + p).wait_recv()
         values = inc_all[c]
         first = (mine * half + c * CHUNK, (1 - mine) * half + c * CHUNK)
         group = min(512, row_count)
@@ -310,17 +340,35 @@
             rows = pl.ds(j * group, group)
             acc[rows, :] = acc[rows, :] + place(slot_col, values, first, rows)
 
-    @pl.loop(0, chunks + LAGS[3])
+    def drain(c):
+        first_kind = c % 2 == 1
+        send_rows(c, upper).wait_send()
+        send_inc(c).wait_send()
+        for stream in (ZA, YA):
+            for copy in send_code(stream, c):
+                copy.wait_send()
+
+        @pl.when(is_odd == first_kind)
+        def _():
+            for copy in send_code(ZB, c):
+                copy.wait_send()
+
+        @pl.when(is_even == first_kind)
+        def _():
+            for copy in send_code(YB, c):
+                copy.wait_send()
+
+    @pl.loop(0, pieces + LAGS[3])
     def _(t):
-        @pl.when(t < chunks)
-        def _():
-            first_hop(t)
-
-        @pl.when((t >= LAGS[0]) & (t < chunks + LAGS[0]))
+        @pl.when((t % cuts == 0) & (t < pieces))
+        def _():
+            first_hop(t // cuts)
+
+        @pl.when((t >= LAGS[0]) & (t < pieces + LAGS[0]))
         def _():
             second_hop(t - LAGS[0])
 
-        @pl.when((t >= LAGS[1]) & (t < chunks + LAGS[1]))
+        @pl.when((t >= LAGS[1]) & (t < pieces + LAGS[1]))
         def _():
             third_hop(t - LAGS[1])
 
@@ -337,32 +385,17 @@
                 slot_col[rows, :] = block.T
             acc[...] = jnp.zeros_like(acc)
 
-        @pl.when((t >= LAGS[2]) & (t < chunks + LAGS[2]))
+        @pl.when((t >= LAGS[2]) & (t < pieces + LAGS[2]))
         def _():
             finish(t - LAGS[2])
 
+        @pl.when((t >= LAGS[3]) & ((t - LAGS[3]) % cuts == cuts - 1))
+        def _():
+            spread((t - LAGS[3]) // cuts)
+
         @pl.when(t >= LAGS[3])
         def _():
-            spread(t - LAGS[3])
-
-    @pl.loop(0, chunks)
-    def _(c):
-        first_kind = c % 2 == 0
-        send_rows(c, upper).wait_send()
-        send_inc(c).wait_send()
-        for stream in (ZA, YA):
-            for copy in send_code(stream, c):
-                copy.wait_send()
-
-        @pl.when(is_odd == first_kind)
-        def _():
-            for copy in send_code(ZB, c):
-                copy.wait_send()
-
-        @pl.when(is_even == first_kind)
-        def _():
-            for copy in send_code(YB, c):
-                copy.wait_send()
+            drain(t - LAGS[3])
 
 
 def shards(amplitudes, integrals, pair_index, partner, occ_energy, vir_energy):
@@ -370,6 +403,7 @@
     row_half = lax.axis_size("row") // 2
     col_count = lax.axis_size("col")
     chunks = row_count // 2 // CHUNK
+    pieces = row_count // 2 // PIECE
     dma = pltpu.SemaphoreType.DMA
     return pl.pallas_call(
         functools.partial(kernel, chunks, width, row_half, col_count),
@@ -388,26 +422,26 @@
             pltpu.VMEM((1, row_count), jnp.int32),
             pltpu.VMEM((1, row_count), F32),
             pltpu.VMEM((1, width), F32),
-            pltpu.VMEM((chunks, CHUNK, width), BF16),
-            pltpu.VMEM((2, chunks, CHUNK, width), BF16),
-            pltpu.VMEM((STOPS, chunks, CHUNK, width), F32),
-            pltpu.VMEM((CHUNK, width), F32),
-            pltpu.VMEM((chunks, CHUNK, 1), F32),
-            pltpu.VMEM((4, chunks, CHUNK, width), jnp.int16),
-            pltpu.VMEM((4, chunks, CHUNK, width), jnp.int16),
-            pltpu.VMEM((4, chunks, 1, width), F32),
-            pltpu.VMEM((4, chunks, 1, width), F32),
-            pltpu.VMEM((chunks, CHUNK, width), BF16),
+            pltpu.VMEM((pieces, PIECE, width), BF16),
+            pltpu.VMEM((2, pieces, PIECE, width), BF16),
+            pltpu.VMEM((STOPS, pieces, PIECE, width), F32),
+            pltpu.VMEM((PIECE, width), F32),
+            pltpu.VMEM((pieces, PIECE, 1), F32),
+            pltpu.VMEM((4, pieces, PIECE, width), jnp.int16),
+            pltpu.VMEM((4, pieces, PIECE, width), jnp.int16),
+            pltpu.VMEM((4, pieces, 1, width), F32),
+            pltpu.VMEM((4, pieces, 1, width), F32),
+            pltpu.VMEM((pieces, PIECE, width), BF16),
             pltpu.VMEM((chunks, 2 * CHUNK, width), BF16),
             dma((6,)),
-            dma((chunks,)),
-            dma((chunks,)),
-            dma((4, chunks)),
-            dma((4, chunks)),
-            dma((4, chunks)),
-            dma((4, chunks)),
-            dma((chunks,)),
-            dma((chunks,)),
+            dma((pieces,)),
+            dma((pieces,)),
+            dma((4, pieces)),
+            dma((4, pieces)),
+            dma((4, pieces)),
+            dma((4, pieces)),
+            dma((pieces,)),
+            dma((pieces,)),
         ],
         compiler_params=pltpu.CompilerParams(
             collective_id=0, has_side_effects=True, vmem_limit_bytes=48 * 1024 * 1024

time: 71 us -> 69.5 us (0.979)
  Pallas kernels: 69.5 us -> 68.1 us
    pallas_call x1, Pallas kernels: 69.5 us -> 68.1 us  [shards(): pl.pallas_call(functools.partial(kernel, chunks, width, row_half, col_cou...]
where the time goes in v3:
time: 69.5 us; the launch traced here: 69.4 us
  Pallas kernels  68.1 us (98%)
  local copies, waits for them, and re-layouts  1.32 us (2%)
    pallas_call x1, Pallas kernels, shards(): pl.pallas_call(functools.partial(kernel, chunks, width, row_half, col_cou...  68.1 us

profile of v3, /device:TPU:6, one launch (start us, length us, event | category | flops | bytes accessed | tf_op | source)
XLA Modules:
  0.0 69.4 jit_solution(10970132565309777156)
XLA Ops:
  0.0 68.1 %shard_map.64 = bf16[2048,512]{1,0:T(8,128)(2,1)S(1)} custom-call(bf16[2048,512]{1,0:T(8,128)(2,1)} %amp_hbm.1, bf16[512,2048]{1,0:T(8,128)(2,1)} %integ_hbm.1, s32[1,2048]{1,0:T(1,128)} %bitcast.4, s32[1,2048]{1,0:T(1,128)} %bitcast.5, f32[1,200]{1,0:T(1,128)} %bitcast.7, f32[1,2000]{1,0:T(1,128)} %bitcast.6), custom_call_target="tpu_custom_call" | custom-call | tf_op jit(solution)/shard_map/pallas_call | solution.py:408
  68.1 1.3 %copy.8 = bf16[2048,512]{1,0:T(8,128)(2,1)} copy(bf16[2048,512]{1,0:T(8,128)(2,1)S(1)} %shard_map.64) | data formatting | bytes 4194304

commit v4 on v3

--- a/solution.py
+++ b/solution.py
@@ -12,6 +12,7 @@
 STOPS = 4
 CHUNK = 128
 PIECE = 64
+LOADS = 4
 LAGS = (3, 6, 9, 13)
 ZA, YA, ZB, YB = range(4)
 LEVELS = 32767.0
@@ -112,20 +113,17 @@
     col_down = (col + col_count - 2) % col_count
     col_flip = col + 1 - 2 * odd
 
+    part_rows = row_count // LOADS
+    slices = [pl.ds(i * part_rows, part_rows) for i in range(LOADS)]
+    moves = [(partner_hbm, partner_row)]
+    moves += [(amp_hbm.at[rows], amp.at[rows]) for rows in slices]
+    moves += [(pair_hbm, pair_row), (occ_hbm, occ_table), (vir_hbm, vir_table)]
+    moves += [(integ_hbm, integ)]
     loads = [
         pltpu.make_async_copy(source, target, load_sem.at[i])
-        for i, (source, target) in enumerate(
-            (
-                (partner_hbm, partner_row),
-                (amp_hbm, amp),
-                (pair_hbm, pair_row),
-                (occ_hbm, occ_table),
-                (vir_hbm, vir_table),
-                (integ_hbm, integ),
-            )
-        )
+        for i, (source, target) in enumerate(moves)
     ]
-    for load in loads[:-1]:
+    for load in loads[: 1 + LOADS]:
         load.start()
 
     barrier = pltpu.get_barrier_semaphore()
@@ -160,7 +158,7 @@
             device_id=peer,
             device_id_type=MESH,
         )
-        return data, scale
+        return scale, data
 
     def send_inc(c):
         return pltpu.make_async_remote_copy(
@@ -195,25 +193,20 @@
         partner_row[...] - partner * row_count,
         iota((1, row_count), 1),
     )
-    loads[1].wait()
-    loads[-1].start()
-    def ready_rows(c):
-        found = own_rows(picks((1 - mine) * half + c * CHUNK))
-        for p in range(cuts):
-            rows_send[c * cuts + p] = found[p * PIECE : (p + 1) * PIECE]
-
-    ready_rows(0)
+    for load in loads[1 : 1 + LOADS]:
+        load.wait()
+    for load in loads[1 + LOADS :]:
+        load.start()
+    rows_send[0] = own_rows(picks((1 - mine) * half))
     pl.semaphore_wait(barrier, 4)
-    for p in range(cuts):
-        send_rows(p, upper).start()
+    send_rows(0, upper).start()
 
     @pl.loop(1, chunks)
     def _(c):
-        ready_rows(c)
-        for p in range(cuts):
-            send_rows(c * cuts + p, upper).start()
-
-    for load in loads[2:]:
+        rows_send[c] = own_rows(picks((1 - mine) * half + c * CHUNK))
+        send_rows(c, upper).start()
+
+    for load in loads[1 + LOADS :]:
         load.wait()
     tile = 256
     right = iota((tile, tile), 1)
@@ -230,13 +223,10 @@
 
     def first_hop(c):
         choice = picks(mine * half + c * CHUNK)
-        own = own_rows(choice)
-        for p in range(cuts):
-            rows_all[upper, c * cuts + p] = own[p * PIECE : (p + 1) * PIECE]
-        for p in range(cuts):
-            send_rows(c * cuts + p, 1 - upper).wait_recv()
-        low = rows_all[0, pl.ds(c * cuts, cuts)].reshape(CHUNK, width)
-        high = rows_all[1, pl.ds(c * cuts, cuts)].reshape(CHUNK, width)
+        rows_all[upper, c] = own_rows(choice)
+        send_rows(c, 1 - upper).wait_recv()
+        low = rows_all[0, c]
+        high = rows_all[1, c]
 
         def multiply(s):
             cols = pl.ds(s * width, width)
@@ -342,8 +332,12 @@
 
     def drain(c):
         first_kind = c % 2 == 1
-        send_rows(c, upper).wait_send()
         send_inc(c).wait_send()
+
+        @pl.when(c % cuts == 0)
+        def _():
+            send_rows(c // cuts, upper).wait_send()
+
         for stream in (ZA, YA):
             for copy in send_code(stream, c):
                 copy.wait_send()
@@ -422,8 +416,8 @@
             pltpu.VMEM((1, row_count), jnp.int32),
             pltpu.VMEM((1, row_count), F32),
             pltpu.VMEM((1, width), F32),
-            pltpu.VMEM((pieces, PIECE, width), BF16),
-            pltpu.VMEM((2, pieces, PIECE, width), BF16),
+            pltpu.VMEM((chunks, CHUNK, width), BF16),
+            pltpu.VMEM((2, chunks, CHUNK, width), BF16),
             pltpu.VMEM((STOPS, pieces, PIECE, width), F32),
             pltpu.VMEM((PIECE, width), F32),
             pltpu.VMEM((pieces, PIECE, 1), F32),
@@ -433,9 +427,9 @@
             pltpu.VMEM((4, pieces, 1, width), F32),
             pltpu.VMEM((pieces, PIECE, width), BF16),
             pltpu.VMEM((chunks, 2 * CHUNK, width), BF16),
-            dma((6,)),
-            dma((pieces,)),
-            dma((pieces,)),
+            dma((5 + LOADS,)),
+            dma((chunks,)),
+            dma((chunks,)),
             dma((4, pieces)),
             dma((4, pieces)),
             dma((4, pieces)),

time: 69.5 us -> 69.4 us (level)
  no operation moved by 1% of the time
where the time goes in v4:
time: 69.4 us; the launch traced here: 69.2 us
  Pallas kernels  67.9 us (98%)
  local copies, waits for them, and re-layouts  1.32 us (2%)
    pallas_call x1, Pallas kernels, shards(): pl.pallas_call(functools.partial(kernel, chunks, width, row_half, col_cou...  67.9 us

profile of v4, /device:TPU:6, one launch (start us, length us, event | category | flops | bytes accessed | tf_op | source)
XLA Modules:
  0.0 69.2 jit_solution(788638652080658652)
XLA Ops:
  0.0 67.9 %shard_map.64 = bf16[2048,512]{1,0:T(8,128)(2,1)S(1)} custom-call(bf16[2048,512]{1,0:T(8,128)(2,1)} %amp_hbm.1, bf16[512,2048]{1,0:T(8,128)(2,1)} %integ_hbm.1, s32[1,2048]{1,0:T(1,128)} %bitcast.4, s32[1,2048]{1,0:T(1,128)} %bitcast.5, f32[1,200]{1,0:T(1,128)} %bitcast.7, f32[1,2000]{1,0:T(1,128)} %bitcast.6), custom_call_target="tpu_custom_call" | custom-call | tf_op jit(solution)/shard_map/pallas_call | solution.py:402
  67.9 1.3 %copy.8 = bf16[2048,512]{1,0:T(8,128)(2,1)} copy(bf16[2048,512]{1,0:T(8,128)(2,1)S(1)} %shard_map.64) | data formatting | bytes 4194304

commit v5 on v4

--- a/solution.py
+++ b/solution.py
@@ -13,7 +13,7 @@
 CHUNK = 128
 PIECE = 64
 LOADS = 4
-LAGS = (3, 6, 9, 13)
+LAGS = (2, 5, 9, 14)
 ZA, YA, ZB, YB = range(4)
 LEVELS = 32767.0
 MESH = pl.DeviceIdType.MESH
@@ -49,9 +49,7 @@
 def place(slot_ref, inc, first, rows):
     at = slot_ref[rows, :]
     lane = iota(at.shape, 1)
-    near = jnp.where(at == lane + first[0], 1.0, 0.0)
-    far = jnp.where(at == lane + first[1], 1.0, 0.0)
-    one_hot = jnp.concatenate([near, far], axis=1).astype(BF16)
+    one_hot = jnp.where(at == lane + first, 1.0, 0.0).astype(BF16)
     return jnp.dot(one_hot, inc, preferred_element_type=F32).astype(BF16)
 
 
@@ -320,15 +318,13 @@
         send_inc(c).start()
         inc_all[c // cuts, pl.ds(c % cuts * PIECE, PIECE)] = jnp.where(is_upper, mirrored, plain).astype(BF16)
 
-    def spread(c):
-        for p in range(cuts):
-            send_inc(c * cuts + p).wait_recv()
-        values = inc_all[c]
-        first = (mine * half + c * CHUNK, (1 - mine) * half + c * CHUNK)
+    def spread(c, side):
+        values = inc_all[c, pl.ds(side * CHUNK, CHUNK)]
+        owner = mine if side == 0 else 1 - mine
         group = min(512, row_count)
         for j in range(row_count // group):
             rows = pl.ds(j * group, group)
-            acc[rows, :] = acc[rows, :] + place(slot_col, values, first, rows)
+            acc[rows, :] = acc[rows, :] + place(slot_col, values, owner * half + c * CHUNK, rows)
 
     def drain(c):
         first_kind = c % 2 == 1
@@ -383,9 +379,15 @@
         def _():
             finish(t - LAGS[2])
 
+        @pl.when((t >= LAGS[2]) & (t < pieces + LAGS[2]) & ((t - LAGS[2]) % cuts == cuts - 1))
+        def _():
+            spread((t - LAGS[2]) // cuts, 0)
+
         @pl.when((t >= LAGS[3]) & ((t - LAGS[3]) % cuts == cuts - 1))
         def _():
-            spread((t - LAGS[3]) // cuts)
+            for p in range(cuts):
+                send_inc((t - LAGS[3]) // cuts * cuts + p).wait_recv()
+            spread((t - LAGS[3]) // cuts, 1)
 
         @pl.when(t >= LAGS[3])
         def _():

time: 69.4 us -> 70 us (level)
  no operation moved by 1% of the time
where the time goes in v5:
time: 70 us; the launch traced here: 69.9 us
  Pallas kernels  68.5 us (98%)
  local copies, waits for them, and re-layouts  1.32 us (2%)
    pallas_call x1, Pallas kernels, shards(): pl.pallas_call(functools.partial(kernel, chunks, width, row_half, col_cou...  68.5 us

profile of v5, /device:TPU:6, one launch (start us, length us, event | category | flops | bytes accessed | tf_op | source)
XLA Modules:
  0.0 69.9 jit_solution(2359332847640304184)
XLA Ops:
  0.0 68.5 %shard_map.64 = bf16[2048,512]{1,0:T(8,128)(2,1)S(1)} custom-call(bf16[2048,512]{1,0:T(8,128)(2,1)} %amp_hbm.1, bf16[512,2048]{1,0:T(8,128)(2,1)} %integ_hbm.1, s32[1,2048]{1,0:T(1,128)} %bitcast.4, s32[1,2048]{1,0:T(1,128)} %bitcast.5, f32[1,200]{1,0:T(1,128)} %bitcast.7, f32[1,2000]{1,0:T(1,128)} %bitcast.6), custom_call_target="tpu_custom_call" | custom-call | tf_op jit(solution)/shard_map/pallas_call | solution.py:404
  68.5 1.3 %copy.8 = bf16[2048,512]{1,0:T(8,128)(2,1)} copy(bf16[2048,512]{1,0:T(8,128)(2,1)S(1)} %shard_map.64) | data formatting | bytes 4194304
